TPU v7x, 256 devices: a whole 4x4x8 slice. The times are simulated.
256 devices in a mesh: pipe: 8 (over y, core), expert: 32 (over x, z).
Axes of the slice: x: 4, y: 4, z: 8, core: 2. Of those that a mesh axis runs over, the one named last changes fastest.
Arguments:
- state: bfloat16 [8, 1536, 2048], P('pipe', 'expert'), may hold values from -6 to 6
- route_ids: int32 [3, 8, 1536, 8], P(None, 'pipe', 'expert'), may hold values from 0 to 31, all different within a row; in each aligned block of 48 rows (0 to 47, 48 to 95, ..., all dimensions but the last counted through in order) at most 16 rows name the same one
- route_weights: float32 [3, 8, 1536, 8], P(None, 'pipe', 'expert'), may hold values from 0.02 to 0.3
- norm_gain: float32 [8, 2048], P('pipe'), may hold values from 0.1 to 1.9
- w_gate: bfloat16 [8, 32, 2048, 768], P('pipe', 'expert'), may hold values from -0.125 to 0.125
- w_up: bfloat16 [8, 32, 2048, 768], P('pipe', 'expert'), may hold values from -0.125 to 0.125
- w_down: bfloat16 [8, 32, 768, 2048], P('pipe', 'expert'), may hold values from -0.21875 to 0.21875
Outputs:
- final_state: bfloat16 [8, 1536, 2048], P('pipe', 'expert')
Inputs may be any that keep to these rules, and one draw needn't show every extreme that they name: `route_ids`: each token names 8 different experts. In the routes of one device (a block of 48 tokens of one step and section) no expert is named more than 16 times, and in every draw some block names an expert exactly 16 times.
All inputs are finite; a program needn't handle non-finite values.
Results may differ from a plain program's by a relative error of at most 0.0065.
Values may be sent and summed in bfloat16 or wider, within the bound.
No kernel may reach another device: no remote copies, remote signals or barrier semaphores. Data moves between devices by JAX's collectives and lax.ppermute only.
A program may use at most 64 MiB of HBM per device.

v0:
```python
import jax
import jax.numpy as jnp
from jax import lax
from jax.sharding import PartitionSpec as P


def shifted(array, axis, by):
    size = lax.axis_size(axis)
    return lax.ppermute(array, axis, [(i, (i + by) % size) for i in range(size)])


def expert_ffn(rows, gate_weight, up_weight, down_weight):
    shape = rows.shape
    flat = rows.reshape(-1, shape[-1])
    gate = jnp.dot(flat, gate_weight, preferred_element_type=jnp.float32)
    upper = jnp.dot(flat, up_weight, preferred_element_type=jnp.float32)
    hidden = (jax.nn.silu(gate) * upper).astype(jnp.bfloat16)
    output = jnp.dot(hidden, down_weight, preferred_element_type=jnp.float32).astype(jnp.bfloat16)
    return output.reshape(shape[:-1] + (down_weight.shape[1],))


def shards(state, route_ids, route_weights, norm_gain, w_gate, w_up, w_down):
    experts = lax.axis_size("expert")
    owner = lax.axis_index("expert")
    panel_rows = state.shape[1]
    width = state.shape[2]
    chosen = route_ids.shape[3]
    capacity = min(panel_rows, 4 * panel_rows * chosen // (3 * experts))
    gain = norm_gain[0]
    gate_weight = w_gate[0, 0]
    up_weight = w_up[0, 0]
    down_weight = w_down[0, 0]
    panel = state[0]
    for tick_index in range(route_ids.shape[0]):
        section_ids = route_ids[tick_index, 0]
        section_wts = route_weights[tick_index, 0]
        widened = panel.astype(jnp.float32)
        scale = lax.rsqrt(jnp.mean(widened * widened, axis=-1, keepdims=True) + 1e-06)
        normed = (widened * scale * gain).astype(jnp.bfloat16)
        matches = (section_ids.reshape(-1)[:, None] == jnp.arange(experts, dtype=jnp.int32)).astype(
            jnp.int32
        )
        ranks = jnp.cumsum(matches, axis=0) - 1
        slot_of = jnp.sum(ranks * matches, axis=1)
        position = section_ids.reshape(-1) * capacity + slot_of
        all_rows, all_ids = (
            lax.all_gather(normed, "expert", axis=0, tiled=True),
            lax.all_gather(section_ids, "expert", axis=0, tiled=True),
        )
        hit_token = jnp.sum((all_ids == owner).astype(jnp.int32), axis=1)
        hit_blocks = hit_token.reshape(experts, panel_rows)
        block_rank = jnp.cumsum(hit_blocks, axis=1) - 1
        sources = jnp.arange(experts, dtype=jnp.int32)[:, None]
        target = jnp.where(
            hit_blocks > 0, sources * capacity + block_rank, experts * capacity
        ).reshape(-1)
        every_token = jnp.arange(experts * panel_rows, dtype=jnp.int32)
        slot_token = (
            jnp.zeros((experts * capacity,), jnp.int32).at[target].set(every_token, mode="drop")
        )
        filled = jnp.zeros((experts * capacity,), jnp.int32).at[target].set(1, mode="drop")
        incoming = jnp.where(filled[:, None] > 0, all_rows[slot_token], jnp.zeros((), jnp.bfloat16))
        results = expert_ffn(
            incoming.reshape(experts, capacity, width), gate_weight, up_weight, down_weight
        )
        returned = lax.all_to_all(results, "expert", split_axis=0, concat_axis=0, tiled=True)
        picked = returned.reshape(experts * capacity, width)[position].reshape(
            panel_rows, chosen, width
        )
        combined = jnp.sum(section_wts[:, :, None] * picked.astype(jnp.float32), axis=1)
        updated = (widened + combined).astype(jnp.bfloat16)
        panel = shifted(updated, "pipe", 1)
    return panel[None]


def solution(mesh):
    placed = (
        P("pipe", "expert", None),
        P(None, "pipe", "expert", None),
        P(None, "pipe", "expert", None),
        P("pipe", None),
        P("pipe", "expert", None, None),
        P("pipe", "expert", None, None),
        P("pipe", "expert", None, None),
    )
    return jax.shard_map(
        shards, mesh=mesh, in_specs=placed, out_specs=P("pipe", "expert", None), check_vma=False
    )
```

profile of v0, /device:TPU:32, one launch (start us, length us, event | category | flops | bytes accessed | tf_op | source)
XLA Modules:
  0.0 707.4 jit_solution(3878133319197394416)
XLA Ops:
  6.5 1.2 fusion.56
  7.8 1.7 fusion.58
  9.5 0.7 slice_bitcast_fusion.3
  10.5 52.2 %all-gather.1 = s32[1,1,1536,8]{3,1,0,2:T(1,128)S(1)} all-gather(s32[1,1,48,8]{3,1,0,2:T(1,128)S(1)} %copy.36), channel_id=3, replica_groups=mesh['pipe'=8,'expert'=32] {'expert'}, dimensions={2}, use_global_device_ids=true | all-gather | bytes 50688 | tf_op jit(solution)/shard_map/all_gather | solution.py:48
  62.7 49.0 %all-gather = s32[1,1,1536,8]{3,1,0,2:T(1,128)S(1)} all-gather(s32[1,1,48,8]{3,1,0,2:T(1,128)S(1)} %copy.35), channel_id=2, replica_groups=mesh['pipe'=8,'expert'=32] {'expert'}, dimensions={2}, use_global_device_ids=true | all-gather | bytes 50688 | tf_op jit(solution)/shard_map/all_gather | solution.py:48
  111.7 63.2 %fusion.42 = (s32[1536]{0:T(1024)S(1)}, s32[1536]{0:T(1024)S(1)}) fusion(s32[1,1,1536,8]{3,1,0,2:T(1,128)S(1)} %all-gather, s32[]{:T(128)S(6)} %axis_index.12, s32[1,1,1536,8]{3,1,0,2:T(1,128)S(1)} %all-gather.1), kind=kLoop, calls=%fused_computation.48 | loop fusion | flops 70656 | bytes 110596 | tf_op jit(solution)/shard_map/reduce_sum | solution.py:50
  175.4 48.6 %all-gather.2 = s32[1,1,1536,8]{3,1,0,2:T(1,128)S(1)} all-gather(s32[1,1,48,8]{3,1,0,2:T(1,128)S(1)} %copy.37), channel_id=4, replica_groups=mesh['pipe'=8,'expert'=32] {'expert'}, dimensions={2}, use_global_device_ids=true | all-gather | bytes 50688 | tf_op jit(solution)/shard_map/all_gather | solution.py:48
  224.0 27.3 %fusion.44 = s32[1536]{0:T(1024)S(1)} fusion(s32[1,1,1536,8]{3,1,0,2:T(1,128)S(1)} %all-gather.2, s32[]{:T(128)S(6)} %axis_index.12), kind=kLoop, calls=%fused_computation.50 | loop fusion | flops 35328 | bytes 55300 | tf_op jit(solution)/shard_map/reduce_sum | solution.py:50
  251.8 6.2 scatter_custom_fusion.1
  258.0 6.4 scatter_custom_fusion
  264.4 8.8 %gather_fusion = bf16[512,2048]{1,0:T(8,128)(2,1)} fusion(bf16[1536,2048]{1,0:T(8,128)(2,1)} %all-gather.7.cloned.1.call-done, s32[1024]{0:T(1024)S(1)} %pad_clamp_fusion.5), kind=kCustom, calls=%fused_computation | custom fusion | bytes 4196352 | tf_op jit(solution)/shard_map/gather | solution.py:62
  273.2 5.5 fusion.19
  278.8 8.3 %fusion.21 = bf16[512,2048]{1,0:T(8,128)(2,1)} fusion(bf16[1,1,768,2048]{3,2,1,0:T(8,128)(2,1)S(1)} %copy-done, f32[512,768]{1,0:T(8,128)} %fusion.19, bf16[1,1,2048,768]{3,2,1,0:T(8,128)(2,1)} %param.12, bf16[512,2048]{1,0:T(8,128)(2,1)} %gather_fusion, pred[512]{0:T(512)(128)(4,1)S(1)} %broadcast_compare_fusion.5), kind=kOutput, calls=%fused_computation.39 | convolution fusion | flops 3225681920 | bytes 12059136 | tf_op jit(solution)/shard_map/dot_general | solution.py:18
  287.1 7.3 %all-to-all-start = ((bf16[32,16,2048]{2,1,0:T(8,128)(2,1)}), bf16[32,16,2048]{2,1,0:T(8,128)(2,1)}, u32[]{:S(2)}, u32[]{:S(2)}) async-start(bf16[32,16,2048]{2,1,0:T(8,128)(2,1)} %bitcast.127), calls=%async_computation | async-start | bytes 4194304 | tf_op jit(solution)/shard_map/all_to_all | solution.py:66
  295.0 1.1 reduce-window.20
  296.2 0.2 slice_reduce_fusion.2
  296.6 27.9 %all-to-all-done = bf16[32,16,2048]{2,1,0:T(8,128)(2,1)} async-done(((bf16[32,16,2048]{2,1,0:T(8,128)(2,1)}), bf16[32,16,2048]{2,1,0:T(8,128)(2,1)}, u32[]{:S(2)}, u32[]{:S(2)}) %all-to-all-start) | async-done | bytes 2097184 | tf_op jit(solution)/shard_map/all_to_all | solution.py:66
  324.5 6.9 gather_fusion.1
  331.4 2.9 fusion.2
  334.4 6.3 collective-permute-done
  340.8 0.8 fusion.50
  341.8 6.2 scatter_custom_fusion.2
  348.0 6.2 scatter_custom_fusion.3
  354.2 71.4 %all-gather.9.cloned.1.call-done = bf16[1536,2048]{1,0:T(8,128)(2,1)} async-done(((bf16[48,2048]{1,0:T(8,128)(2,1)}), bf16[1536,2048]{1,0:T(8,128)(2,1)}) %all-gather.9.cloned.1.call-update) | async-done | bytes 6291472 | tf_op jit(solution)/shard_map/all_gather | solution.py:47
  425.6 9.3 %gather_fusion.2 = bf16[512,2048]{1,0:T(8,128)(2,1)} fusion(bf16[1536,2048]{1,0:T(8,128)(2,1)} %all-gather.9.cloned.1.call-done, s32[1024]{0:T(1024)S(1)} %pad_clamp_fusion.3), kind=kCustom, calls=%fused_computation.2 | custom fusion | bytes 4196352 | tf_op jit(solution)/shard_map/gather | solution.py:62
  434.9 5.5 fusion.17
  440.4 8.3 %fusion.24 = bf16[512,2048]{1,0:T(8,128)(2,1)} fusion(bf16[1,1,768,2048]{3,2,1,0:T(8,128)(2,1)S(1)} %copy-done, f32[512,768]{1,0:T(8,128)} %fusion.17, bf16[1,1,2048,768]{3,2,1,0:T(8,128)(2,1)} %param.12, bf16[512,2048]{1,0:T(8,128)(2,1)} %gather_fusion.2, pred[512]{0:T(512)(128)(4,1)S(1)} %broadcast_compare_fusion.4), kind=kOutput, calls=%fused_computation.40 | convolution fusion | flops 3225681920 | bytes 12059136 | tf_op jit(solution)/shard_map/dot_general | solution.py:18
  448.8 5.8 all-to-all-start.1
  455.2 1.1 reduce-window.24
  456.2 0.2 slice_reduce_fusion.1
  456.6 47.4 %all-to-all-done.1 = bf16[32,16,2048]{2,1,0:T(8,128)(2,1)} async-done(((bf16[32,16,2048]{2,1,0:T(8,128)(2,1)}), bf16[32,16,2048]{2,1,0:T(8,128)(2,1)}, u32[]{:S(2)}, u32[]{:S(2)}) %all-to-all-start.1) | async-done | bytes 2097184 | tf_op jit(solution)/shard_map/all_to_all | solution.py:66
  504.0 6.9 gather_fusion.3
  510.9 2.9 fusion.1
  513.9 6.3 collective-permute-done.1
  520.3 0.8 fusion.54
  521.3 6.2 scatter_custom_fusion.4
  527.5 6.2 scatter_custom_fusion.5
  533.7 72.1 %all-gather.11.cloned.1.call-done = bf16[1536,2048]{1,0:T(8,128)(2,1)} async-done(((bf16[48,2048]{1,0:T(8,128)(2,1)}), bf16[1536,2048]{1,0:T(8,128)(2,1)}) %all-gather.11.cloned.1.call-update) | async-done | bytes 6291472 | tf_op jit(solution)/shard_map/all_gather | solution.py:47
  605.8 9.0 %gather_fusion.4 = bf16[512,2048]{1,0:T(8,128)(2,1)} fusion(bf16[1536,2048]{1,0:T(8,128)(2,1)} %all-gather.11.cloned.1.call-done, s32[1024]{0:T(1024)S(1)} %pad_clamp_fusion.1), kind=kCustom, calls=%fused_computation.4 | custom fusion | bytes 4196352 | tf_op jit(solution)/shard_map/gather | solution.py:62
  614.9 5.5 fusion.15
  620.4 8.3 %fusion.27 = bf16[512,2048]{1,0:T(8,128)(2,1)} fusion(bf16[1,1,768,2048]{3,2,1,0:T(8,128)(2,1)S(1)} %copy-done, f32[512,768]{1,0:T(8,128)} %fusion.15, bf16[1,1,2048,768]{3,2,1,0:T(8,128)(2,1)} %param.12, bf16[512,2048]{1,0:T(8,128)(2,1)} %gather_fusion.4, pred[512]{0:T(512)(128)(4,1)S(1)} %broadcast_compare_fusion.3), kind=kOutput, calls=%fused_computation.41 | convolution fusion | flops 3225681920 | bytes 12059136 | tf_op jit(solution)/shard_map/dot_general | solution.py:18
  628.7 5.8 all-to-all-start.2
  635.1 0.9 reduce-window.26
  636.4 47.3 %all-to-all-done.2 = bf16[32,16,2048]{2,1,0:T(8,128)(2,1)} async-done(((bf16[32,16,2048]{2,1,0:T(8,128)(2,1)}), bf16[32,16,2048]{2,1,0:T(8,128)(2,1)}, u32[]{:S(2)}, u32[]{:S(2)}) %all-to-all-start.2) | async-done | bytes 2097184 | tf_op jit(solution)/shard_map/all_to_all | solution.py:66
  683.7 6.9 gather_fusion.5
  690.6 2.9 fusion
  693.6 6.3 collective-permute-done.2
  699.9 0.7 copy.51
  (94 shorter events, 4.5 us)
Async XLA Ops:
  6.5 272.2 %copy-start = (bf16[1,1,768,2048]{3,2,1,0:T(8,128)(2,1)S(1)}, bf16[1,1,768,2048]{3,2,1,0:T(8,128)(2,1)}, u32[]{:S(2)}) copy-start(bf16[1,1,768,2048]{3,2,1,0:T(8,128)(2,1)} %param.13) | copy-start | bytes 9437188
  6.5 257.9 %all-gather.7.cloned.1.call-start = ((), (), s32[]{:S(2)}) async-start(), calls=%async_computation.3 | async-start | bytes 6488064 | tf_op jit(solution)/shard_map/all_gather | solution.py:47
  287.1 7.6 %copy-start.3 = (f32[3,1,48,8]{2,3,1,0:T(8,128)S(1)}, f32[3,1,48,8]{2,3,1,0:T(8,128)}, u32[]{:S(2)}) copy-start(f32[3,1,48,8]{2,3,1,0:T(8,128)} %param.9) | copy-start | bytes 13828
  287.1 37.4 %all-to-all-start = ((bf16[32,16,2048]{2,1,0:T(8,128)(2,1)}), bf16[32,16,2048]{2,1,0:T(8,128)(2,1)}, u32[]{:S(2)}, u32[]{:S(2)}) async-start(bf16[32,16,2048]{2,1,0:T(8,128)(2,1)} %bitcast.127), calls=%async_computation | async-start | bytes 4194304 | tf_op jit(solution)/shard_map/all_to_all | solution.py:66
  294.4 131.2 %all-gather.9.cloned.1.call-start = ((), (), s32[]{:S(2)}) async-start(), calls=%async_computation.4 | async-start | bytes 6488064 | tf_op jit(solution)/shard_map/all_gather | solution.py:47
  331.4 2.9 copy-start.1
  331.4 9.4 %copy-start.2 = (f32[1,2048]{1,0:T(1,128)S(1)}, f32[1,2048]{1,0:T(1,128)}, u32[]{:S(2)}) copy-start(f32[1,2048]{1,0:T(1,128)} %param.10) | copy-start | bytes 24580
  334.4 6.3 collective-permute-start
  448.8 55.2 %all-to-all-start.1 = ((bf16[32,16,2048]{2,1,0:T(8,128)(2,1)}), bf16[32,16,2048]{2,1,0:T(8,128)(2,1)}, u32[]{:S(2)}, u32[]{:S(2)}) async-start(bf16[32,16,2048]{2,1,0:T(8,128)(2,1)} %bitcast.129), calls=%async_computation.1 | async-start | bytes 4194304 | tf_op jit(solution)/shard_map/all_to_all | solution.py:66
  454.6 151.2 %all-gather.11.cloned.1.call-start = ((), (), s32[]{:S(2)}) async-start(), calls=%async_computation.5 | async-start | bytes 6488064 | tf_op jit(solution)/shard_map/all_gather | solution.py:47
  513.9 6.3 collective-permute-start.1
  628.7 55.0 %all-to-all-start.2 = ((bf16[32,16,2048]{2,1,0:T(8,128)(2,1)}), bf16[32,16,2048]{2,1,0:T(8,128)(2,1)}, u32[]{:S(2)}, u32[]{:S(2)}) async-start(bf16[32,16,2048]{2,1,0:T(8,128)(2,1)} %bitcast.128), calls=%async_computation.2 | async-start | bytes 4194304 | tf_op jit(solution)/shard_map/all_to_all | solution.py:66
  693.6 6.3 collective-permute-start.2
Sparse Core Ops, SparseCore 0:
  9.9 92.9 all-gather.6
  341.8 83.7 all-gather.8
  521.3 84.5 all-gather.10
where the time goes:
time: 708 us; the launch traced here: 707 us
  waiting for transfers between devices  285 us (40%)
  blocking collectives  150 us (21%)
  other arithmetic  109 us (15%)
  local copies, waits for them, and re-layouts  89.3 us (13%)
  matrix products  41.6 us (6%)
  starting transfers between devices  19.1 us (3%)
  between operations  13.9 us (2%)
    all_gather x3, blocking collectives, shards(): lax.all_gather(section_ids, 'expert', axis=0, tiled=True)  150 us
    all_gather x3, waiting for transfers between devices, shards(): lax.all_gather(normed, 'expert', axis=0, tiled=True)  144 us
    all_to_all x3, waiting for transfers between devices, shards(): lax.all_to_all(results, 'expert', split_axis=0, concat_axis=0, tiled=True)  123 us
    reduce_sum x2, other arithmetic, shards(): hit_token = jnp.sum((all_ids == owner).astype(jnp.int32), axis=1)  90.4 us
    gather x3, local copies, waits for them, and re-layouts, shards(): all_rows[slot_token]  27.1 us
    dot_general x3, matrix products, expert_ffn(): jnp.dot(hidden, down_weight, preferred_element_type=jnp.float32)  25 us
    gather x3, local copies, waits for them, and re-layouts, shards(): returned.reshape(experts * capacity, width)[position]  20.8 us
    all_to_all x3, starting transfers between devices, shards(): lax.all_to_all(results, 'expert', split_axis=0, concat_axis=0, tiled=True)  19 us
  transfers between devices with their start and end apart: 9, of which 8 were waited for; matrix products, arithmetic and copies ran while one was open for 19% of the time, Pallas kernels for 0%

commit v1 on v0

--- a/solution.py
+++ b/solution.py
@@ -43,8 +43,15 @@
         ranks = jnp.cumsum(matches, axis=0) - 1
         slot_of = jnp.sum(ranks * matches, axis=1)
         position = section_ids.reshape(-1) * capacity + slot_of
+
+        def finish_the_halves(local_values, out_dim):
+            newest = jnp.stack([local_values] * lax.psum(1, axis_name="expert"), axis=0)
+            return jnp.concatenate(
+                lax.all_to_all(newest, axis_name="expert", concat_axis=0, split_axis=0), out_dim
+            )
+
         all_rows, all_ids = (
-            lax.all_gather(normed, "expert", axis=0, tiled=True),
+            finish_the_halves(normed, 0),
             lax.all_gather(section_ids, "expert", axis=0, tiled=True),
         )
         hit_token = jnp.sum((all_ids == owner).astype(jnp.int32), axis=1)

time: 708 us -> 978 us (1.38)
  blocking collectives: 150 us -> 278 us
  waiting for transfers between devices: 285 us -> 394 us
  starting transfers between devices: 19.1 us -> 48.6 us
  between operations: 13.9 us -> 0.75 us
    all_to_all x0 -> x3, waiting for transfers between devices: none -> 253 us  [finish_the_halves(): lax.all_to_all(newest, axis_name='expert', concat_axis=0, split_axis=0)]
    all_gather x3 -> x0, waiting for transfers between devices: 144 us -> none  [shards(): lax.all_gather(normed, 'expert', axis=0, tiled=True)]
    all_gather x3, blocking collectives: 150 us -> 278 us  [shards(): lax.all_gather(section_ids, 'expert', axis=0, tiled=True)]
    all_to_all x0 -> x3, starting transfers between devices: none -> 23.9 us  [finish_the_halves(): lax.all_to_all(newest, axis_name='expert', concat_axis=0, split_axis=0)]
    another operation x3 -> x6, local copies, waits for them, and re-layouts: 0.44 us -> 10.8 us  [the longest x3 10.4 us: finish_the_halves(): newest = jnp.stack([local_values] * lax.psum(1, axis_name='expert'), axis=0)]
  transfers between devices with their start and end apart: 9 -> 9, of which waited for: 8 -> 8; matrix products, arithmetic and copies ran while one was open for 19% -> 14% of each run, Pallas kernels for 0% -> 0%
where the time goes in v1:
time: 978 us; the launch traced here: 973 us
  waiting for transfers between devices  394 us (40%)
  blocking collectives  278 us (28%)
  other arithmetic  112 us (11%)
  local copies, waits for them, and re-layouts  98.6 us (10%)
  starting transfers between devices  48.6 us (5%)
  matrix products  41.6 us (4%)
    all_gather x3, blocking collectives, shards(): lax.all_gather(section_ids, 'expert', axis=0, tiled=True)  278 us
    all_to_all x3, waiting for transfers between devices, finish_the_halves(): lax.all_to_all(newest, axis_name='expert', concat_axis=0, split_axis=0)  253 us
    all_to_all x3, waiting for transfers between devices, shards(): lax.all_to_all(results, 'expert', split_axis=0, concat_axis=0, tiled=True)  122 us
    reduce_sum x2, other arithmetic, shards(): hit_token = jnp.sum((all_ids == owner).astype(jnp.int32), axis=1)  96.4 us
    gather x3, local copies, waits for them, and re-layouts, shards(): all_rows[slot_token]  26.9 us
    dot_general x3, matrix products, expert_ffn(): jnp.dot(hidden, down_weight, preferred_element_type=jnp.float32)  25 us
    all_to_all x3, starting transfers between devices, shards(): lax.all_to_all(results, 'expert', split_axis=0, concat_axis=0, tiled=True)  24.6 us
    all_to_all x3, starting transfers between devices, finish_the_halves(): lax.all_to_all(newest, axis_name='expert', concat_axis=0, split_axis=0)  23.9 us
  transfers between devices with their start and end apart: 9, of which 8 were waited for; matrix products, arithmetic and copies ran while one was open for 14% of the time, Pallas kernels for 0%

profile of v1, /device:TPU:32, one launch (start us, length us, event | category | flops | bytes accessed | tf_op | source)
XLA Modules:
  0.0 973.4 jit_solution(12512370641007549305)
XLA Ops:
  0.0 1.2 fusion.50
  1.2 1.1 fusion.62
  2.3 3.5 stack.9
  5.7 11.4 %all-to-all-start = ((bf16[32,48,2048]{2,1,0:T(8,128)(2,1)}), bf16[32,48,2048]{2,1,0:T(8,128)(2,1)}, u32[]{:S(2)}, u32[]{:S(2)}) async-start(bf16[32,48,2048]{2,1,0:T(8,128)(2,1)} %stack.9), calls=%async_computation | async-start | bytes 12582912 | tf_op jit(solution)/shard_map/all_to_all | solution.py:50
  17.4 181.7 %all-gather.1 = s32[1,1,1536,8]{3,1,0,2:T(1,128)S(1)} all-gather(s32[1,1,48,8]{3,1,0,2:T(1,128)S(1)} %copy.36), channel_id=3, replica_groups=mesh['pipe'=8,'expert'=32] {'expert'}, dimensions={2}, use_global_device_ids=true | all-gather | bytes 50688 | tf_op jit(solution)/shard_map/all_gather | solution.py:55
  199.0 47.6 %all-gather = s32[1,1,1536,8]{3,1,0,2:T(1,128)S(1)} all-gather(s32[1,1,48,8]{3,1,0,2:T(1,128)S(1)} %copy.35), channel_id=2, replica_groups=mesh['pipe'=8,'expert'=32] {'expert'}, dimensions={2}, use_global_device_ids=true | all-gather | bytes 50688 | tf_op jit(solution)/shard_map/all_gather | solution.py:55
  246.6 69.1 %fusion.42 = (s32[1536]{0:T(1024)S(1)}, s32[1536]{0:T(1024)S(1)}) fusion(s32[1,1,1536,8]{3,1,0,2:T(1,128)S(1)} %all-gather, s32[]{:T(128)S(6)} %axis_index.12, s32[1,1,1536,8]{3,1,0,2:T(1,128)S(1)} %all-gather.1), kind=kLoop, calls=%fused_computation.48 | loop fusion | flops 70656 | bytes 110596 | tf_op jit(solution)/shard_map/reduce_sum | solution.py:57
  316.3 48.6 %all-gather.2 = s32[1,1,1536,8]{3,1,0,2:T(1,128)S(1)} all-gather(s32[1,1,48,8]{3,1,0,2:T(1,128)S(1)} %copy.37), channel_id=4, replica_groups=mesh['pipe'=8,'expert'=32] {'expert'}, dimensions={2}, use_global_device_ids=true | all-gather | bytes 50688 | tf_op jit(solution)/shard_map/all_gather | solution.py:55
  364.9 27.3 %fusion.44 = s32[1536]{0:T(1024)S(1)} fusion(s32[1,1,1536,8]{3,1,0,2:T(1,128)S(1)} %all-gather.2, s32[]{:T(128)S(6)} %axis_index.12), kind=kLoop, calls=%fused_computation.50 | loop fusion | flops 35328 | bytes 55300 | tf_op jit(solution)/shard_map/reduce_sum | solution.py:57
  392.7 6.2 scatter_custom_fusion.1
  398.9 6.3 scatter_custom_fusion
  405.3 8.8 gather_fusion
  414.1 5.5 fusion.19
  419.6 8.3 fusion.21
  427.9 8.3 all-to-all-start.1
  436.8 0.9 reduce-window.20
  438.0 28.0 %all-to-all-done.1 = bf16[32,16,2048]{2,1,0:T(8,128)(2,1)} async-done(((bf16[32,16,2048]{2,1,0:T(8,128)(2,1)}), bf16[32,16,2048]{2,1,0:T(8,128)(2,1)}, u32[]{:S(2)}, u32[]{:S(2)}) %all-to-all-start.1) | async-done | bytes 2097184 | tf_op jit(solution)/shard_map/all_to_all | solution.py:73
  466.0 6.9 gather_fusion.1
  473.0 2.9 fusion.2
  476.0 6.3 collective-permute-done
  482.6 3.5 stack.10
  486.0 5.3 all-to-all-start.2
  491.4 6.2 scatter_custom_fusion.2
  497.6 6.2 scatter_custom_fusion.3
  503.8 125.8 %all-to-all-done.2 = bf16[32,48,2048]{2,1,0:T(8,128)(2,1)} async-done(((bf16[32,48,2048]{2,1,0:T(8,128)(2,1)}), bf16[32,48,2048]{2,1,0:T(8,128)(2,1)}, u32[]{:S(2)}, u32[]{:S(2)}) %all-to-all-start.2) | async-done | bytes 6291488 | tf_op jit(solution)/shard_map/all_to_all | solution.py:50
  629.6 9.2 gather_fusion.2
  638.8 5.5 fusion.17
  644.3 8.3 fusion.24
  652.7 7.7 all-to-all-start.3
  660.9 0.9 reduce-window.24
  662.2 47.2 %all-to-all-done.3 = bf16[32,16,2048]{2,1,0:T(8,128)(2,1)} async-done(((bf16[32,16,2048]{2,1,0:T(8,128)(2,1)}), bf16[32,16,2048]{2,1,0:T(8,128)(2,1)}, u32[]{:S(2)}, u32[]{:S(2)}) %all-to-all-start.3) | async-done | bytes 2097184 | tf_op jit(solution)/shard_map/all_to_all | solution.py:73
  709.4 6.9 gather_fusion.3
  716.3 2.9 fusion.1
  719.3 6.3 collective-permute-done.1
  725.8 3.5 stack.11
  729.3 7.3 all-to-all-start.4
  736.7 6.2 scatter_custom_fusion.4
  742.9 6.2 scatter_custom_fusion.5
  749.1 126.8 %all-to-all-done.4 = bf16[32,48,2048]{2,1,0:T(8,128)(2,1)} async-done(((bf16[32,48,2048]{2,1,0:T(8,128)(2,1)}), bf16[32,48,2048]{2,1,0:T(8,128)(2,1)}, u32[]{:S(2)}, u32[]{:S(2)}) %all-to-all-start.4) | async-done | bytes 6291488 | tf_op jit(solution)/shard_map/all_to_all | solution.py:50
  875.9 8.8 gather_fusion.4
  884.7 5.5 fusion.15
  890.2 8.3 fusion.27
  898.6 8.7 all-to-all-start.5
  907.8 0.9 reduce-window.26
  909.1 47.2 %all-to-all-done.5 = bf16[32,16,2048]{2,1,0:T(8,128)(2,1)} async-done(((bf16[32,16,2048]{2,1,0:T(8,128)(2,1)}), bf16[32,16,2048]{2,1,0:T(8,128)(2,1)}, u32[]{:S(2)}, u32[]{:S(2)}) %all-to-all-start.5) | async-done | bytes 2097184 | tf_op jit(solution)/shard_map/all_to_all | solution.py:73
  956.3 6.9 gather_fusion.5
  963.3 2.9 fusion
  966.2 6.3 collective-permute-done.2
  (96 shorter events, 5.7 us)
Async XLA Ops:
  0.0 419.6 %copy-start = (bf16[1,1,768,2048]{3,2,1,0:T(8,128)(2,1)S(1)}, bf16[1,1,768,2048]{3,2,1,0:T(8,128)(2,1)}, u32[]{:S(2)}) copy-start(bf16[1,1,768,2048]{3,2,1,0:T(8,128)(2,1)} %param.13) | copy-start | bytes 9437188
  5.7 11.4 %copy-start.4 = (s32[3,1,48,8]{2,3,1,0:T(8,128)S(1)}, s32[3,1,48,8]{2,3,1,0:T(8,128)}, u32[]{:S(2)}) copy-start(s32[3,1,48,8]{2,3,1,0:T(8,128)} %param.8) | copy-start | bytes 13828
  5.7 399.5 %all-to-all-start = ((bf16[32,48,2048]{2,1,0:T(8,128)(2,1)}), bf16[32,48,2048]{2,1,0:T(8,128)(2,1)}, u32[]{:S(2)}, u32[]{:S(2)}) async-start(bf16[32,48,2048]{2,1,0:T(8,128)(2,1)} %stack.9), calls=%async_computation | async-start | bytes 12582912 | tf_op jit(solution)/shard_map/all_to_all | solution.py:50
  427.9 8.5 copy-start.3
  427.9 38.1 %all-to-all-start.1 = ((bf16[32,16,2048]{2,1,0:T(8,128)(2,1)}), bf16[32,16,2048]{2,1,0:T(8,128)(2,1)}, u32[]{:S(2)}, u32[]{:S(2)}) async-start(bf16[32,16,2048]{2,1,0:T(8,128)(2,1)} %bitcast.137), calls=%async_computation.1 | async-start | bytes 4194304 | tf_op jit(solution)/shard_map/all_to_all | solution.py:73
  473.0 2.9 copy-start.1
  473.0 9.4 copy-start.2
  476.0 6.3 collective-permute-start
  486.0 143.6 %all-to-all-start.2 = ((bf16[32,48,2048]{2,1,0:T(8,128)(2,1)}), bf16[32,48,2048]{2,1,0:T(8,128)(2,1)}, u32[]{:S(2)}, u32[]{:S(2)}) async-start(bf16[32,48,2048]{2,1,0:T(8,128)(2,1)} %stack.10), calls=%async_computation.2 | async-start | bytes 12582912 | tf_op jit(solution)/shard_map/all_to_all | solution.py:50
  652.7 56.7 %all-to-all-start.3 = ((bf16[32,16,2048]{2,1,0:T(8,128)(2,1)}), bf16[32,16,2048]{2,1,0:T(8,128)(2,1)}, u32[]{:S(2)}, u32[]{:S(2)}) async-start(bf16[32,16,2048]{2,1,0:T(8,128)(2,1)} %bitcast.139), calls=%async_computation.3 | async-start | bytes 4194304 | tf_op jit(solution)/shard_map/all_to_all | solution.py:73
  719.2 6.3 collective-permute-start.1
  729.3 146.6 %all-to-all-start.4 = ((bf16[32,48,2048]{2,1,0:T(8,128)(2,1)}), bf16[32,48,2048]{2,1,0:T(8,128)(2,1)}, u32[]{:S(2)}, u32[]{:S(2)}) async-start(bf16[32,48,2048]{2,1,0:T(8,128)(2,1)} %stack.11), calls=%async_computation.4 | async-start | bytes 12582912 | tf_op jit(solution)/shard_map/all_to_all | solution.py:50
  898.6 57.8 %all-to-all-start.5 = ((bf16[32,16,2048]{2,1,0:T(8,128)(2,1)}), bf16[32,16,2048]{2,1,0:T(8,128)(2,1)}, u32[]{:S(2)}, u32[]{:S(2)}) async-start(bf16[32,16,2048]{2,1,0:T(8,128)(2,1)} %bitcast.138), calls=%async_computation.5 | async-start | bytes 4194304 | tf_op jit(solution)/shard_map/all_to_all | solution.py:73
  966.2 6.3 collective-permute-start.2
